TPU v7x, 32 devices: a whole 2x2x4 slice. The times are simulated.
32 devices in a mesh: tmpl: 4 (over y, core), seq: 2 (over x), tp: 4 (over z).
Axes of the slice: x: 2, y: 2, z: 4, core: 2. Of those that a mesh axis runs over, the one named last changes fastest.
Arguments:
- tokens: bfloat16 [3072, 5376], P(('tmpl', 'seq', 'tp')), parts along dimension 0, may hold values from -6 to 6
- lengths: int32 [8], P('tmpl'), parts along dimension 0, may hold values from 1 to 384, as said below
- input_gain: float32 [5376], replicated, may hold values from 0.1 to 1.9
- query_proj: bfloat16 [5376, 512], P(None, 'tp'), may hold values from -0.078125 to 0.078125
- key_value: bfloat16 [5376, 1024], P(None, 'tp'), may hold values from -0.078125 to 0.078125
- query_gain: float32 [128], replicated, may hold values from 0.5 to 20, as said below
- key_gain: float32 [128], replicated, may hold values from 0.5 to 6, as said below
- window_cache: bfloat16 [4096, 1024], P(('tmpl', 'seq'), 'tp'), parts along dimension 0, may hold values from -6 to 6
- output_proj: bfloat16 [512, 5376], P('tp', 'seq'), may hold values from -0.25 to 0.25
- post_gain: float32 [5376], replicated, may hold values from 0.1 to 1.9
Outputs:
- layer_out: bfloat16 [3072, 5376], P(('tmpl', 'seq', 'tp')), parts along dimension 0
There are 4 independent parts, one for each index of `tmpl`. A program takes and returns all parts, laid end to end along the dimension named above; an argument that names none is the same for every part. Nothing has to cross between parts.
Inputs may be any that keep to these rules, and one draw needn't show every extreme that they name: The template's live slab tokens fill the first lengths[s] slots of seq index s, in order of s; one entry equals 384. `query_gain`: positive entries. `key_gain`: positive entries.
All inputs are finite; a program needn't handle non-finite values.
Results may differ from a plain program's by a relative error of at most 0.018.
The roundings to bfloat16 on the way count: a program that leaves them out, or rounds other values in their place, can miss the bound.
Values may be sent and summed in bfloat16 or wider, within the bound.
A program may use at most 64 MiB of HBM per device.

v0:
```python
import jax
import jax.numpy as jnp
from jax import lax
from jax.sharding import PartitionSpec as P

WIN = 1024
PREFIX = 32768


EPSILON = 1e-06
ROPE_BASE = 10000.0
QUERY_SCALE = 168.0 ** (-0.5)
MASKED = -1e30


def normalize(values, scale_gain):
    values = values.astype(jnp.float32)
    return (
        values * lax.rsqrt(jnp.mean(values * values, axis=-1, keepdims=True) + EPSILON) * scale_gain
    )


def rotate(values, positions):
    half_width = values.shape[-1] // 2
    frequency = jnp.power(
        ROPE_BASE, -2.0 * jnp.arange(half_width, dtype=jnp.float32) / values.shape[-1]
    )
    angles = positions.astype(jnp.float32)[:, None] * frequency[None, :]
    cosine_table = jnp.cos(angles)
    sine_table = jnp.sin(angles)
    first_half = values[:, :half_width]
    second_half = values[:, half_width:]
    return jnp.concatenate(
        [
            first_half * cosine_table - second_half * sine_table,
            second_half * cosine_table + first_half * sine_table,
        ],
        axis=1,
    )


def shards(
    tokens,
    lengths,
    input_gain,
    query_proj,
    key_value,
    query_gain,
    key_gain,
    window_cache,
    output_proj,
    post_gain,
):
    row_count = tokens.shape[0]
    slab_slots = row_count * lax.axis_size("tp")
    head_width = query_proj.shape[1]
    cache_slots = window_cache.shape[0]
    block_rows = slab_slots + cache_slots
    shard_count = lengths.shape[0]
    shard_index = lax.axis_index("seq")
    normed = normalize(tokens, input_gain).astype(jnp.bfloat16)
    piece = lax.all_gather(normed, "tp", axis=0, tiled=True)
    projected = jnp.concatenate(
        [
            jnp.dot(piece, query_proj, preferred_element_type=jnp.float32),
            jnp.dot(piece, key_value, preferred_element_type=jnp.float32),
        ],
        axis=1,
    )
    offsets = jnp.cumsum(lengths) - lengths
    shard_ids = jnp.arange(shard_count, dtype=jnp.int32)
    own_length = jnp.sum(jnp.where(shard_ids == shard_index, lengths, 0))
    own_offset = jnp.sum(jnp.where(shard_ids == shard_index, offsets, 0))
    slot_index = jnp.arange(slab_slots, dtype=jnp.int32)
    positions = PREFIX + own_offset + slot_index
    live_rows = slot_index < own_length
    queries = (
        rotate(normalize(projected[:, :head_width], query_gain), positions) * QUERY_SCALE
    ).astype(jnp.bfloat16)
    new_keys = rotate(
        normalize(projected[:, head_width : 2 * head_width], key_gain), positions
    ).astype(jnp.bfloat16)
    new_values = projected[:, 2 * head_width :].astype(jnp.bfloat16)
    own_block = jnp.concatenate(
        [jnp.concatenate([new_keys, new_values], axis=1), window_cache], axis=0
    )
    gathered = lax.all_gather(own_block, "seq", axis=0, tiled=True)
    running_max = jnp.full((slab_slots,), MASKED, jnp.float32)
    key_rows = gathered[:, :head_width]
    value_rows = gathered[:, head_width:]
    key_index = 0 + jnp.arange(gathered.shape[0], dtype=jnp.int32)
    key_shard = key_index // block_rows
    inner_row = key_index % block_rows
    picked = key_shard[:, None] == shard_ids[None, :]
    shard_offset = jnp.sum(jnp.where(picked, offsets[None, :], 0), axis=1)
    shard_length = jnp.sum(jnp.where(picked, lengths[None, :], 0), axis=1)
    in_slab = inner_row < slab_slots
    key_position = jnp.where(
        in_slab,
        PREFIX + shard_offset + inner_row,
        PREFIX - WIN + key_shard * cache_slots + inner_row - slab_slots,
    )
    key_live = jnp.where(in_slab, inner_row < shard_length, True)
    key_position, key_live = (key_position, key_live)
    visible = (
        key_live[None, :]
        & (key_position[None, :] <= positions[:, None])
        & (key_position[None, :] > positions[:, None] - WIN)
    )
    scores = lax.dot_general(
        queries, key_rows, (((1,), (1,)), ((), ())), preferred_element_type=jnp.float32
    )
    scores = jnp.where(visible, scores, MASKED)
    new_max = jnp.maximum(running_max, jnp.max(scores, axis=1))
    weights = jnp.where(visible, jnp.exp(scores - new_max[:, None]), 0.0)
    running_sum = jnp.sum(weights, axis=1)
    running_acc = jnp.dot(
        weights.astype(jnp.bfloat16), value_rows, preferred_element_type=jnp.float32
    )
    head_out = running_acc / jnp.where(live_rows, running_sum, 1.0)[:, None]
    head_out = jnp.where(live_rows[:, None], head_out, 0.0).astype(jnp.bfloat16)
    full_weights = lax.all_gather(output_proj, "seq", axis=1, tiled=True)
    projection = lax.psum_scatter(
        jnp.dot(head_out, full_weights, preferred_element_type=jnp.float32).astype(jnp.bfloat16),
        "tp",
        scatter_dimension=0,
        tiled=True,
    ).astype(jnp.float32)
    post_norm = normalize(projection, post_gain)
    return (tokens.astype(jnp.float32) + post_norm).astype(jnp.bfloat16)


def solution(mesh):
    return jax.shard_map(
        shards,
        mesh=mesh,
        in_specs=(
            P(("tmpl", "seq", "tp"), None),
            P("tmpl"),
            P(),
            P(None, "tp"),
            P(None, "tp"),
            P(),
            P(),
            P(("tmpl", "seq"), "tp"),
            P("tp", "seq"),
            P(),
        ),
        out_specs=P(("tmpl", "seq", "tp"), None),
        check_vma=False,
    )
```

profile of v0, /device:TPU:0, one launch (start us, length us, event | category | flops | bytes accessed | tf_op | source)
XLA Modules:
  0.0 221.9 jit_solution(13530554699072405083)
XLA Ops:
  6.5 0.0 copy-start
  6.5 0.0 copy-start.7
  6.5 0.0 all-gather.3.cloned.1.call-start
  6.5 1.7 fusion.2
  8.2 2.5 %fusion.4 = bf16[96,5376]{1,0:T(8,128)(2,1)} fusion(bf16[96,5376]{1,0:T(8,128)(2,1)} %param.10, f32[5376]{0:T(1024)} %param.12, f32[96]{0:T(128)S(1)} %add_rsqrt_fusion.3), kind=kLoop, calls=%fused_computation.13 | loop fusion | flops 2064384 | bytes 2086272 | tf_op jit(solution)/shard_map/convert_element_type | solution.py:61
  10.7 0.0 all-gather.3.cloned.1.call-update
  10.8 0.0 all-gather.5.cloned.1.call-start
  10.8 0.7 all-gather.5.cloned.1.call-update
  11.5 0.0 reduce-scatter.2.cloned.1.call-start
  11.6 0.0 copy-done.7
  11.6 0.2 reduce-window.9
  11.8 0.7 fusion.57
  13.2 0.6 iota_compare_fusion.1
  13.8 0.1 select_reduce_fusion.1
  14.0 79.3 %all-gather.3.cloned.1.call-done = bf16[384,5376]{1,0:T(8,128)(2,1)} async-done(((bf16[96,5376]{1,0:T(8,128)(2,1)}), bf16[384,5376]{1,0:T(8,128)(2,1)}) %all-gather.3.cloned.1.call-update) | async-done | bytes 4128784 | tf_op jit(solution)/shard_map/all_gather | solution.py:62
  93.3 0.0 copy-done
  93.3 0.0 copy-start.1
  93.3 0.0 copy-start.3
  93.3 4.0 %fusion.63 = f32[384,256]{0,1:T(8,128)S(1)} fusion(bf16[384,5376]{1,0:T(8,128)(2,1)} %all-gather.3.cloned.1.call-done, bf16[5376,256]{1,0:T(8,128)(2,1)S(1)} %copy-done), kind=kOutput, calls=%fused_computation.91 | convolution fusion | flops 1056964608 | bytes 7274496 | tf_op jit(solution)/shard_map/dot_general | solution.py:66
  97.3 0.0 copy-done.1
  97.3 0.0 copy-done.3
  97.3 0.0 copy-start.8
  97.3 0.0 copy-start.9
  97.4 0.0 copy-start.5
  97.4 1.3 multiply_reduce_fusion.1
  98.7 0.0 copy-done.8
  98.7 0.0 copy-done.9
  98.7 0.1 multiply_multiply_fusion
  98.8 1.1 fusion.35
  100.0 0.1 copy.12
  100.1 0.0 copy-done.5
  100.2 23.1 %all_gather.10 = bf16[1792,256]{1,0:T(8,128)(2,1)S(1)} all-gather(bf16[896,256]{1,0:T(8,128)(2,1)S(1)} %pad_maximum_fusion), channel_id=1, replica_groups=mesh['tmpl'=4,'seq'=2,'tp'=4] {'seq'}, dimensions={0}, use_global_device_ids=true | all-gather | bytes 1376256 | tf_op jit(solution)/shard_map/all_gather | solution.py:87
  123.3 0.0 copy-start.4
  123.3 0.9 copy-done.4
  124.2 2.0 fusion.62
  126.3 0.0 copy-start.2
  126.3 1.5 copy-done.2
  127.8 1.2 fusion.6
  129.0 0.6 broadcast_select_fusion
  129.7 0.0 all-gather.5.cloned.1.call-done
  129.7 6.9 %convolution_convert_fusion = bf16[384,5376]{1,0:T(8,128)(2,1)} fusion(bf16[128,5376]{1,0:T(8,128)(2,1)} %all-gather.5.cloned.1.call-done, f32[384,1792]{1,0:T(8,128)} %copy-done.2, f32[384]{0:T(512)S(1)} %broadcast_maximum_fusion, bf16[1792,256]{1,0:T(8,128)(2,1)} %copy-done.4, f32[384]{0:T(512)S(1)} %broadcast_select_fusion, ...), kind=kOutput, calls=%fused_computation | convolution fusion | flops 711671808 | bytes 8731776 | tf_op jit(solution)/shard_map/dot_general | solution.py:124
  136.6 0.0 copy-start.6
  136.6 0.0 reduce-scatter.2.cloned.1.call-update
  136.6 74.3 %reduce-scatter.2.cloned.1.call-done = bf16[96,5376]{1,0:T(8,128)(2,1)} async-done(((bf16[384,5376]{1,0:T(8,128)(2,1)}), bf16[96,5376]{1,0:T(8,128)(2,1)}) %reduce-scatter.2.cloned.1.call-update) | async-done | bytes 1032208 | tf_op jit(solution)/shard_map/reduce_scatter | solution.py:123
  210.9 1.5 fusion
  212.4 0.0 copy-done.6
  212.4 2.9 %fusion.5 = bf16[96,5376]{1,0:T(8,128)(2,1)} fusion(bf16[96,5376]{1,0:T(8,128)(2,1)} %reduce-scatter.2.cloned.1.call-done, bf16[96,5376]{1,0:T(8,128)(2,1)} %param.10, f32[5376]{0:T(1024)S(1)} %copy-done.6, f32[96]{0:T(128)S(1)} %add_rsqrt_fusion.2), kind=kLoop, calls=%fused_computation.14 | loop fusion | flops 3096576 | bytes 3118464 | tf_op jit(solution)/shard_map/convert_element_type | solution.py:130
  (15 shorter events, 0.2 us)
Async XLA Ops:
  6.5 86.8 %copy-start = (bf16[5376,256]{1,0:T(8,128)(2,1)S(1)}, bf16[5376,256]{1,0:T(8,128)(2,1)}, u32[]{:S(2)}) copy-start(bf16[5376,256]{1,0:T(8,128)(2,1)} %param.14) | copy-start | bytes 8257540
  6.5 5.0 %copy-start.7 = (s32[2]{0:T(128)S(1)}, s32[2]{0:T(128)}, u32[]{:S(2)}) copy-start(s32[2]{0:T(128)} %param.11) | copy-start | bytes 28
  6.5 86.8 %all-gather.3.cloned.1.call-start = ((), (), s32[]{:S(2)}) async-start(), calls=%async_computation.1 | async-start | bytes 5160960 | tf_op jit(solution)/shard_map/all_gather | solution.py:62
  10.8 118.9 %all-gather.5.cloned.1.call-start = ((), (), s32[]{:S(2)}) async-start(), calls=%async_computation.2 | async-start | bytes 2064384 | tf_op jit(solution)/shard_map/all_gather | solution.py:122
  11.5 199.4 %reduce-scatter.2.cloned.1.call-start = ((), (), s32[]{:S(2)}) async-start(), calls=%async_computation.3 | async-start | bytes 5160960 | tf_op jit(solution)/shard_map/reduce_scatter | solution.py:123
  93.3 4.0 %copy-start.1 = (bf16[384,5376]{1,0:T(8,128)(2,1)S(1)}, bf16[384,5376]{1,0:T(8,128)(2,1)}, u32[]{:S(2)}) copy-start(bf16[384,5376]{1,0:T(8,128)(2,1)} %all-gather.3.cloned.1.call-done) | copy-start | bytes 12386308
  93.3 4.0 %copy-start.3 = (bf16[5376,128]{1,0:T(8,128)(2,1)S(1)}, bf16[5376,128]{1,0:T(8,128)(2,1)}, u32[]{:S(2)}) copy-start(bf16[5376,128]{1,0:T(8,128)(2,1)} %param.13) | copy-start | bytes 4128772
  97.3 1.4 copy-start.8
  97.3 1.4 copy-start.9
  97.4 2.8 %copy-start.5 = (bf16[512,256]{1,0:T(8,128)(2,1)S(1)}, bf16[512,256]{1,0:T(8,128)(2,1)}, u32[]{:S(2)}) copy-start(bf16[512,256]{1,0:T(8,128)(2,1)} %param.17) | copy-start | bytes 786436
  123.3 0.9 copy-start.4
  126.3 1.5 copy-start.2
  136.6 75.8 %copy-start.6 = (f32[5376]{0:T(1024)S(1)}, f32[5376]{0:T(1024)}, u32[]{:S(2)}) copy-start(f32[5376]{0:T(1024)} %param.19) | copy-start | bytes 64516
Sparse Core Ops, SparseCore 0:
  10.9 82.3 all-gather.2
  94.8 33.0 all-gather.4
  136.7 74.1 reduce-scatter.1
where the time goes:
time: 222 us
  waiting for transfers between devices  154 us (69%)
  blocking collectives  23.1 us (10%)
  matrix products  14.2 us (6%)
  between operations  14 us (6%)
  other arithmetic  13.5 us (6%)
  local copies, waits for them, and re-layouts  2.63 us (1%)
    all_gather x1, waiting for transfers between devices, shards(): piece = lax.all_gather(normed, 'tp', axis=0, tiled=True)  79.3 us
    reduce_scatter x1, waiting for transfers between devices, shards(): lax.psum_scatter(jnp.dot(head_out, full_weights, preferred_element_type=j...  74.3 us
    all_gather x1, blocking collectives, shards(): gathered = lax.all_gather(own_block, 'seq', axis=0, tiled=True)  23.1 us
    dot_general x1, matrix products, shards(): jnp.dot(head_out, full_weights, preferred_element_type=jnp.float32)  6.89 us
  transfers between devices with their start and end apart: 3, of which 2 were waited for; matrix products, arithmetic and copies ran while one was open for 6% of the time, Pallas kernels for 0%

commit v1 on v0

v1 whole, which is shorter than its diff:
```python
import functools

import jax
import jax.numpy as jnp
from jax import lax
from jax.experimental import pallas as pl
from jax.experimental.pallas import tpu as pltpu
from jax.sharding import PartitionSpec as P

WIN = 1024
PREFIX = 32768
EPSILON = 1e-06
ROPE_BASE = 10000.0
QUERY_SCALE = 168.0 ** (-0.5)
MASKED = -1e30
F32 = jnp.float32
BF16 = jnp.bfloat16
MESH = pl.DeviceIdType.MESH


def chunk_of(width, limit):
    best = 128
    for c in range(128, limit + 1, 128):
        if width % c == 0:
            best = c
    return best


def flat(v):
    shape = (v.shape[0] * v.shape[1], v.shape[2])
    if v.shape[1] % 16 == 0:
        return v.reshape(shape)
    return v.astype(F32).reshape(shape).astype(v.dtype)


def kernel(
    T, S, N, S2,
    lengths, tokens, wq_hbm, wkv_hbm, cache_hbm, oproj_hbm,
    igain, pgain, qgain, kgain, cos_t, sin_t,
    out_ref,
    xbuf, nbuf, wq, wkv, cbuf, og, q_all, kv_all, q_snd, kv_snd, hsnd, ho, proj,
    lsem, ssem, hssem,
    r_x, r_c, r_w, r_oz, r_op, r_q, r_kv, r_kvx, r_h, r_own,
):
    t, s, z = lax.axis_index("tmpl"), lax.axis_index("seq"), lax.axis_index("tp")
    h = N // 2
    p, b = z // h, z % h
    zp = (z + h) % N
    R, D = tokens.shape
    HW = wq_hbm.shape[1]
    C = cache_hbm.shape[0]
    DE = D // (T * S2)
    OR = oproj_hbm.shape[0] // T
    DC = oproj_hbm.shape[1]
    tc = t + 1 - 2 * (t % 2)
    par = t % 2
    ys = [(t + 2 * k) % T for k in range(1, T // 2)]
    xs = [(s + k) % S for k in range(1, S)]
    sg, sb = (s // S2) * S2, s % S2
    x2 = [(sb + k) % S2 for k in range(1, S2)]
    zs = [(z + k) % N for k in range(1, N)]

    pending = []

    def send(src, dst, rsem, dev):
        c = pltpu.make_async_remote_copy(
            src_ref=src, dst_ref=dst, send_sem=ssem.at[len(pending)], recv_sem=rsem,
            device_id=dev, device_id_type=MESH,
        )
        c.start()
        pending.append(c)

    def arrived(dst, rsem):
        pltpu.make_async_remote_copy(
            src_ref=dst, dst_ref=dst, send_sem=ssem.at[0], recv_sem=rsem,
            device_id={"tp": zp}, device_id_type=MESH,
        ).wait_recv()

    loc = [
        pltpu.make_async_copy(tokens, xbuf.at[b], lsem.at[0]),
        pltpu.make_async_copy(wq_hbm, wq.at[0], lsem.at[1]),
        pltpu.make_async_copy(wkv_hbm, wkv.at[0], lsem.at[2]),
        pltpu.make_async_copy(cache_hbm, cbuf.at[s], lsem.at[3]),
        pltpu.make_async_copy(
            oproj_hbm.at[pl.ds(pl.multiple_of(t * OR, OR), OR)], og.at[s, t, z], lsem.at[4]
        ),
    ]
    for c in loc:
        c.start()

    barrier = pltpu.get_barrier_semaphore()
    peers = (
        [{"tp": k} for k in zs] + [{"seq": k} for k in xs]
        + [{"tmpl": k} for k in ys] + [{"tmpl": tc}]
    )
    for dev in peers:
        pl.semaphore_signal(barrier, inc=1, device_id=dev, device_id_type=MESH)
    pl.semaphore_wait(barrier, len(peers))

    def piece(e_t, e_s):
        return pl.ds(pl.multiple_of((e_t * S2 + e_s) * DE, DE), DE)

    wset = ((1, wkv_hbm, wkv), (0, wq_hbm, wq))
    for a, src, buf in wset:
        send(src.at[piece(t, sb)], buf.at[1, piece(t, sb)], r_own.at[a], {"tp": zp})
    for k in range(1, h):
        send(tokens, xbuf.at[b], r_x.at[b], {"tp": p * h + (b + k) % h})
    for k in zs:
        send(
            oproj_hbm.at[pl.ds(pl.multiple_of(t * OR, OR), OR)], og.at[s, t, z],
            r_oz.at[z], {"tp": k},
        )
    for k in xs:
        send(cache_hbm, cbuf.at[s], r_c.at[s], {"seq": k})

    RB = 16 if R % 16 == 0 else 8
    KC = chunk_of(D, 1024)

    def norm_rows(slot):
        def body(i, carry):
            rows = pl.ds(pl.multiple_of(i * RB, RB), RB)
            v = xbuf[slot, rows, :].astype(F32)
            inv = lax.rsqrt(jnp.sum(v * v, axis=1, keepdims=True) * (1.0 / D) + EPSILON)
            nbuf[slot, rows, :] = (v * inv * igain[...]).astype(BF16)
            return carry

        lax.fori_loop(0, R // RB, body, 0)

    def head_norm(v, gain):
        inv = lax.rsqrt(jnp.mean(v * v, axis=1, keepdims=True) + EPSILON)
        return v * inv * gain

    def project(slot, j):
        def body(i, acc):
            ks = pl.ds(pl.multiple_of(i * KC, KC), KC)
            xv = nbuf[slot, :, ks]
            return (
                acc[0] + jnp.dot(xv, wq[j, ks, :], preferred_element_type=F32),
                acc[1] + jnp.dot(xv, wkv[j, ks, :], preferred_element_type=F32),
            )

        qr, kv = lax.fori_loop(
            0, D // KC, body, (jnp.zeros((R, HW), F32), jnp.zeros((R, 2 * HW), F32))
        )
        co, si = cos_t[slot], sin_t[slot]

        def rope(u):
            return u * co + pltpu.roll(u, HW // 2, 1) * si

        q = (rope(head_norm(qr, qgain[...])) * QUERY_SCALE).astype(BF16)
        k = rope(head_norm(kv[:, :HW], kgain[...])).astype(BF16)
        return q, jnp.concatenate([k, kv[:, HW:].astype(BF16)], axis=1)

    def own_head(slot):
        q, kv = project(slot, 0)
        n = p * h + slot
        q_all[n] = q
        kv_all[s, n] = kv
        for k in xs:
            send(kv_all.at[s, n], kv_all.at[s, n], r_kvx.at[s, n], {"seq": k})

    def other_head(slot):
        q, kv = project(slot, 1)
        n = p * h + slot
        q_snd[slot] = q
        kv_snd[slot] = kv
        send(kv_snd.at[slot], kv_all.at[s, n], r_kv.at[n], {"tp": zp})
        send(q_snd.at[slot], q_all.at[n], r_q.at[n], {"tp": zp})

    loc[0].wait()
    norm_rows(b)
    loc[1].wait()
    loc[2].wait()
    own_head(b)

    for a, src, buf in wset:
        pc = buf.at[1, piece(t, sb)]
        arrived(pc, r_own.at[a])
        for k in x2:
            send(pc, pc, r_w.at[a, t, sb], {"seq": sg + k})
        for k in ys:
            send(pc, pc, r_w.at[a, t, sb], {"tmpl": k})
        send(pc, pc, r_w.at[a, t, sb], {"tmpl": tc})
    for a, src, buf in wset:
        for k2 in x2:
            pc = buf.at[1, piece(t, k2)]
            arrived(pc, r_w.at[a, t, k2])
            for k in ys:
                send(pc, pc, r_w.at[a, t, k2], {"tmpl": k})
            send(pc, pc, r_w.at[a, t, k2], {"tmpl": tc})
    loc[4].wait()
    for k in zs:
        arrived(og.at[s, t, k], r_oz.at[k])

    def out_send(ps, pt, over_y, over_x):
        pc = og.at[ps, pt]
        if over_x:
            for k in xs:
                send(pc, pc, r_op.at[ps, pt], {"seq": k})
        if over_y:
            for k in ys:
                send(pc, pc, r_op.at[ps, pt], {"tmpl": k})
        send(pc, pc, r_op.at[ps, pt], {"tmpl": tc})

    for a, src, buf in wset:
        for k in ys:
            for k2 in range(S2):
                ks = (sb + k2) % S2
                pc = buf.at[1, piece(k, ks)]
                arrived(pc, r_w.at[a, k, ks])
                send(pc, pc, r_w.at[a, k, ks], {"tmpl": tc})
    out_send(s, t, True, True)

    for k in range(1, h):
        slot = (b + k) % h
        arrived(xbuf.at[slot], r_x.at[slot])
        norm_rows(slot)
        own_head(slot)
    for a, src, buf in wset:
        for k in range(T // 2):
            kt = (1 - par) + 2 * k
            for ks in range(S2):
                arrived(buf.at[1, piece(kt, ks)], r_w.at[a, kt, ks])
    for k in range(h):
        other_head((b + k) % h)

    for k in ys:
        arrived(og.at[s, k], r_op.at[s, k])
        out_send(s, k, False, True)

    op = 1 - p
    for i in range(h):
        n = op * h + i
        arrived(kv_all.at[s, n], r_kv.at[n])
        for k in xs:
            send(kv_all.at[s, n], kv_all.at[s, n], r_kvx.at[s, n], {"seq": k})
    for i in range(h):
        n = op * h + i
        arrived(q_all.at[n], r_q.at[n])
    for k in xs:
        for kt in range(T // 2):
            ot = par + 2 * kt
            arrived(og.at[k, ot], r_op.at[k, ot])
            out_send(k, ot, False, False)
    loc[3].wait()
    for k in xs:
        arrived(cbuf.at[k], r_c.at[k])
        for n in range(N):
            arrived(kv_all.at[k, n], r_kvx.at[k, n])

    lens = [lengths[k] for k in range(S)]
    offs = []
    total = jnp.int32(0)
    for k in range(S):
        offs.append(total)
        total = total + lens[k]
    own_off = jnp.int32(0)
    own_len = jnp.int32(0)
    for k in range(S):
        own_off = own_off + jnp.where(s == k, offs[k], 0)
        own_len = own_len + jnp.where(s == k, lens[k], 0)

    def attend(d, carry):
        n = lax.rem(z + d, N)
        q = q_all[n]
        slot_c = n * R + lax.broadcasted_iota(jnp.int32, (R, 1), 0)
        pos = PREFIX + own_off + slot_c
        scores, allow, values = [], [], []
        for k in range(S):
            cb = cbuf[k]
            sc = lax.dot_general(
                q, cb[:, :HW], (((1,), (1,)), ((), ())), preferred_element_type=F32
            )
            kp = PREFIX - WIN + k * C + lax.broadcasted_iota(jnp.int32, (1, C), 1)
            ok = (kp <= pos) & (kp > pos - WIN)
            scores.append(jnp.where(ok, sc, MASKED))
            allow.append(ok)
            values.append(cb[:, HW:])
            kv = flat(kv_all[k])
            sc = lax.dot_general(
                q, kv[:, :HW], (((1,), (1,)), ((), ())), preferred_element_type=F32
            )
            j = lax.broadcasted_iota(jnp.int32, (1, N * R), 1)
            kp = PREFIX + offs[k] + j
            ok = (kp <= pos) & (kp > pos - WIN) & (j < lens[k])
            scores.append(jnp.where(ok, sc, MASKED))
            allow.append(ok)
            values.append(kv[:, HW:])
        top = functools.reduce(
            jnp.maximum, [jnp.max(v, axis=1, keepdims=True) for v in scores]
        )
        row_sum = jnp.zeros((R, 1), F32)
        acc = jnp.zeros((R, HW), F32)
        for sc, ok, vv in zip(scores, allow, values):
            w = jnp.where(ok, jnp.exp(sc - top), 0.0)
            row_sum = row_sum + jnp.sum(w, axis=1, keepdims=True)
            acc = acc + jnp.dot(w.astype(BF16), vv, preferred_element_type=F32)
        live = slot_c < own_len
        res = acc / jnp.where(live, row_sum, 1.0)
        hsnd[n] = jnp.where(live, res, 0.0).astype(BF16)

        @pl.when(d < N)
        def _():
            pltpu.make_async_remote_copy(
                src_ref=hsnd.at[n], dst_ref=ho.at[z], send_sem=hssem.at[n],
                recv_sem=r_h.at[z], device_id={"tp": n}, device_id_type=MESH,
            ).start()

        return carry

    lax.fori_loop(1, N + 1, attend, 0)
    ho[z] = hsnd[z]

    for k in range(S):
        for kt in range(T // 2):
            ot = (1 - par) + 2 * kt
            arrived(og.at[k, ot], r_op.at[k, ot])
    for k in zs:
        arrived(ho.at[k], r_h.at[k])

    CC = chunk_of(DC, 1024)

    for k in range(S):
        def cols(i, carry):
            cs = pl.ds(pl.multiple_of(i * CC, CC), CC)
            acc = jnp.zeros((R, CC), F32)
            for g in range(N):
                w = jnp.concatenate([og[k, kt, g, :, cs] for kt in range(T)], axis=0)
                acc = acc + jnp.dot(ho[g], w, preferred_element_type=F32).astype(BF16).astype(F32)
            proj[:, pl.ds(pl.multiple_of(k * DC + i * CC, 128), CC)] = acc
            return carry

        lax.fori_loop(0, DC // CC, cols, 0)

    def finish(i, carry):
        rows = pl.ds(pl.multiple_of(i * RB, RB), RB)
        v = proj[rows, :]
        inv = lax.rsqrt(jnp.sum(v * v, axis=1, keepdims=True) * (1.0 / D) + EPSILON)
        out_ref[rows, :] = (xbuf[b, rows, :].astype(F32) + v * inv * pgain[...]).astype(BF16)
        return carry

    lax.fori_loop(0, R // RB, finish, 0)

    for c in pending:
        c.wait_send()
    for k in zs:
        pltpu.make_async_remote_copy(
            src_ref=hsnd.at[k], dst_ref=ho.at[z], send_sem=hssem.at[k],
            recv_sem=r_h.at[z], device_id={"tp": k}, device_id_type=MESH,
        ).wait_send()


def shards(
    T, S, N,
    tokens, lengths, input_gain, query_proj, key_value, query_gain, key_gain,
    window_cache, output_proj, post_gain,
):
    R, D = tokens.shape
    HW = query_proj.shape[1]
    C = window_cache.shape[0]
    h = N // 2
    S2 = max(d for d in range(1, S + 1) if S % d == 0 and D % (16 * T * d) == 0)
    s, z = lax.axis_index("seq"), lax.axis_index("tp")
    own_offset = jnp.sum(jnp.where(jnp.arange(S, dtype=jnp.int32) < s, lengths, 0))
    slot = (z // h) * (h * R) + jnp.arange(h * R, dtype=jnp.int32)
    positions = PREFIX + own_offset + slot
    half = HW // 2
    freq = jnp.power(ROPE_BASE, -2.0 * jnp.arange(half, dtype=F32) / HW)
    angles = positions.astype(F32)[:, None] * freq[None, :]
    co, si = jnp.cos(angles), jnp.sin(angles)
    cos_t = jnp.concatenate([co, co], axis=1).reshape(h, R, HW)
    sin_t = jnp.concatenate([-si, si], axis=1).reshape(h, R, HW)
    OR, DC = output_proj.shape[0] // T, output_proj.shape[1]
    w_sends = 2 * (1 + (S2 - 1 + T // 2) + (S2 - 1) * (T // 2) + (T // 2 - 1) * S2)
    o_sends = (N - 1) + (T // 2 - 1) + (T // 2) * (S - 1) + S * (T // 2)
    sends = w_sends + o_sends + (h - 1) + (S - 1) + N * (S - 1) + 2 * h
    vm = pl.BlockSpec(memory_space=pltpu.VMEM)
    hb = pl.BlockSpec(memory_space=pl.ANY)
    dma = pltpu.SemaphoreType.DMA
    return pl.pallas_call(
        functools.partial(kernel, T, S, N, S2),
        out_shape=jax.ShapeDtypeStruct((R, D), BF16),
        in_specs=[pl.BlockSpec(memory_space=pltpu.SMEM), hb, hb, hb, hb, hb]
        + [vm] * 6,
        out_specs=vm,
        scratch_shapes=[
            pltpu.VMEM((h, R, D), BF16),
            pltpu.VMEM((h, R, D), BF16),
            pltpu.VMEM((2, D, HW), BF16),
            pltpu.VMEM((2, D, 2 * HW), BF16),
            pltpu.VMEM((S, C, 2 * HW), BF16),
            pltpu.VMEM((S, T, N, OR, DC), BF16),
            pltpu.VMEM((N, R, HW), BF16),
            pltpu.VMEM((S, N, R, 2 * HW), BF16),
            pltpu.VMEM((h, R, HW), BF16),
            pltpu.VMEM((h, R, 2 * HW), BF16),
            pltpu.VMEM((N, R, HW), BF16),
            pltpu.VMEM((N, R, HW), BF16),
            pltpu.VMEM((R, D), F32),
            dma((5,)), dma((sends,)), dma((N,)),
            dma((h,)), dma((S,)), dma((2, T, S2)), dma((N,)), dma((S, T)),
            dma((N,)), dma((N,)), dma((S, N)), dma((N,)), dma((2,)),
        ],
        compiler_params=pltpu.CompilerParams(
            collective_id=0, has_side_effects=True, vmem_limit_bytes=60 * 2**20
        ),
    )(
        lengths, tokens, query_proj, key_value, window_cache, output_proj,
        input_gain[None, :], post_gain[None, :], query_gain[None, :], key_gain[None, :],
        cos_t, sin_t,
    )


def solution(mesh):
    T, S, N = mesh.shape["tmpl"], mesh.shape["seq"], mesh.shape["tp"]
    return jax.shard_map(
        functools.partial(shards, T, S, N),
        mesh=mesh,
        in_specs=(
            P(("tmpl", "seq", "tp"), None),
            P("tmpl"),
            P(),
            P(None, "tp"),
            P(None, "tp"),
            P(),
            P(),
            P(("tmpl", "seq"), "tp"),
            P("tp", "seq"),
            P(),
        ),
        out_specs=P(("tmpl", "seq", "tp"), None),
        check_vma=False,
    )
```

time: 222 us -> 105 us (0.47)
  waiting for transfers between devices: 154 us -> 0 us
  Pallas kernels: 0 us -> 96.6 us
  blocking collectives: 23.1 us -> 0 us
  matrix products: 14.2 us -> 0 us
  between operations: 14 us -> 0.68 us
  other arithmetic: 13.5 us -> 2.54 us
  local copies, waits for them, and re-layouts: 2.63 us -> 4.95 us
    pallas_call x0 -> x1, Pallas kernels: none -> 96.6 us  [shards(): pl.pallas_call(functools.partial(kernel, T, S, N, S2), out_shape=jax.Shap...]
    all_gather x2 -> x0, waiting for transfers between devices: 79.3 us -> none  [the longest x1 79.3 us: shards(): piece = lax.all_gather(normed, 'tp', axis=0, tiled=True)]
    reduce_scatter x1 -> x0, waiting for transfers between devices: 74.3 us -> none  [shards(): lax.psum_scatter(jnp.dot(head_out, full_weights, preferred_element_type=j...]
    all_gather x1 -> x0, blocking collectives: 23.1 us -> none  [shards(): gathered = lax.all_gather(own_block, 'seq', axis=0, tiled=True)]
    dot_general x4 -> x0, matrix products: 14.2 us -> none  [the longest x1 6.89 us: shards(): jnp.dot(head_out, full_weights, preferred_element_type=jnp.float32)]
    convert_element_type x3 -> x1, other arithmetic: 5.43 us -> 0.01 us  [shards(): angles = positions.astype(F32)[:, None] * freq[None, :]]
    reduce_sum x6 -> x1, other arithmetic: 5.26 us -> 1.29 us  [shards(): jnp.sum(jnp.where(jnp.arange(S, dtype=jnp.int32) < s, lengths, 0))]
    broadcast_in_dim x0 -> x2, local copies, waits for them, and re-layouts: none -> 2.7 us  [the longest x1 1.35 us: shards(): input_gain[None, :]]
  transfers between devices with their start and end apart: 3 -> 0, of which waited for: 2 -> 0; matrix products, arithmetic and copies ran while one was open for 6% -> 0% of each run, Pallas kernels for 0% -> 0%
where the time goes in v1:
time: 105 us
  Pallas kernels  96.6 us (92%)
  local copies, waits for them, and re-layouts  4.95 us (5%)
  other arithmetic  2.54 us (2%)
    pallas_call x1, Pallas kernels, shards(): pl.pallas_call(functools.partial(kernel, T, S, N, S2), out_shape=jax.Shap...  96.6 us
    unnamed x1, local copies, waits for them, and re-layouts  2.25 us

profile of v1, /device:TPU:0, one launch (start us, length us, event | category | flops | bytes accessed | tf_op | source)
XLA Modules:
  0.0 104.8 jit_solution(4754854312411341818)
XLA Ops:
  0.0 1.3 %fusion.1 = s32[]{:T(128)} fusion(s32[2]{0:T(128)} %lengths.1, s32[]{:T(128)S(6)} %axis_index.23), kind=kLoop, calls=%fused_computation.7 | loop fusion | flops 5 | bytes 16 | tf_op jit(solution)/shard_map/reduce_sum | solution.py:364
  2.0 1.4 %broadcast_in_dim.18.igain = f32[1,5376]{1,0:T(1,128)} reshape(f32[5376]{0:T(1024)} %param.12) | data formatting | bytes 43008 | tf_op jit(solution)/shard_map/broadcast_in_dim | solution.py:409
  3.3 1.4 %broadcast_in_dim.19.pgain = f32[1,5376]{1,0:T(1,128)} reshape(f32[5376]{0:T(1024)} %param.19) | data formatting | bytes 43008 | tf_op jit(solution)/shard_map/broadcast_in_dim | solution.py:409
  4.7 0.4 fusion
  5.1 0.8 pad_maximum_fusion
  5.9 96.6 %shard_map.100 = bf16[96,5376]{1,0:T(8,128)(2,1)} custom-call(s32[2]{0:T(128)} %lengths.1, bf16[96,5376]{1,0:T(8,128)(2,1)} %tokens.1, bf16[5376,128]{1,0:T(8,128)(2,1)} %wq_hbm.1, bf16[5376,256]{1,0:T(8,128)(2,1)} %wkv_hbm.1, bf16[512,256]{1,0:T(8,128)(2,1)} %cache_hbm.1, bf16[128,2688]{1,0:T(8,128)(2,1)} %oproj_hbm.1, f32[1,5376]{1,0:T(1,128)} %broadcast_in_dim.18.igain, ...), custom_call_target="tpu_custom_call" | custom-call | tf_op jit(solution)/shard_map/pallas_call | solution.py:380
  102.5 2.2 %copy.12 = bf16[96,5376]{1,0:T(8,128)(2,1)} copy(bf16[96,5376]{1,0:T(8,128)(2,1)} %shard_map.100) | data formatting | bytes 2064384
  (2 shorter events, 0.0 us)

commit v2 on v1

v2 whole, which is shorter than its diff:
```python
import functools

import jax
import jax.numpy as jnp
import numpy as np
from jax import lax
from jax.experimental import pallas as pl
from jax.experimental.pallas import tpu as pltpu
from jax.sharding import PartitionSpec as P

WIN = 1024
PREFIX = 32768
EPSILON = 1e-06
ROPE_BASE = 10000.0
QUERY_SCALE = 168.0 ** (-0.5)
MASKED = -1e30
F32 = jnp.float32
BF16 = jnp.bfloat16
MESH = pl.DeviceIdType.MESH


def chunk_of(width, limit):
    best = 128
    for c in range(128, limit + 1, 128):
        if width % c == 0:
            best = c
    return best


def flat(v):
    shape = (v.shape[0] * v.shape[1], v.shape[2])
    if v.shape[1] % 16 == 0:
        return v.reshape(shape)
    return v.astype(F32).reshape(shape).astype(v.dtype)


def kernel(
    T, S, N, S2, NC, NG,
    lengths, tokens, wq_hbm, wkv_hbm, cache_hbm, oproj_hbm,
    ig_hbm, pg_hbm, qgain, kgain, freq,
    out_ref,
    igs, pgs, igain, pgain, cos_t, sin_t, xbuf, nbuf, wq, wkv, cbuf, og, q_all, kv_all, q_snd, kv_snd, hsnd, ho, proj,
    lsem, ssem, hssem,
    r_x, r_c, r_w, r_oz, r_o, r_q, r_kv, r_kvx, r_h, r_own,
):
    t, s, z = lax.axis_index("tmpl"), lax.axis_index("seq"), lax.axis_index("tp")
    h = N // 2
    p, b = z // h, z % h
    zp = (z + h) % N
    R, D = tokens.shape
    HW = wq_hbm.shape[1]
    C = cache_hbm.shape[0]
    DE = D // (T * S2)
    OR = oproj_hbm.shape[0] // T
    DC = oproj_hbm.shape[1]
    tc = t + 1 - 2 * (t % 2)
    par = t % 2
    ys = [(t + 2 * k) % T for k in range(1, T // 2)]
    xs = [(s + k) % S for k in range(1, S)]
    sg, sb = (s // S2) * S2, s % S2
    x2 = [(sb + k) % S2 for k in range(1, S2)]
    zs = [(z + k) % N for k in range(1, N)]

    pending = []

    def queue(src, dst, rsem, dev):
        c = pltpu.make_async_remote_copy(
            src_ref=src, dst_ref=dst, send_sem=ssem.at[len(pending)], recv_sem=rsem,
            device_id=dev, device_id_type=MESH,
        )
        pending.append(c)
        return c

    def send(src, dst, rsem, dev):
        queue(src, dst, rsem, dev).start()

    def arrived(dst, rsem):
        pltpu.make_async_remote_copy(
            src_ref=dst, dst_ref=dst, send_sem=ssem.at[0], recv_sem=rsem,
            device_id={"tp": zp}, device_id_type=MESH,
        ).wait_recv()

    loc = [
        pltpu.make_async_copy(tokens, xbuf.at[b], lsem.at[0]),
        pltpu.make_async_copy(wq_hbm, wq.at[0], lsem.at[1]),
        pltpu.make_async_copy(wkv_hbm, wkv.at[0], lsem.at[2]),
        pltpu.make_async_copy(cache_hbm, cbuf.at[s], lsem.at[3]),
        pltpu.make_async_copy(
            oproj_hbm.at[pl.ds(pl.multiple_of(t * OR, OR), OR)], og.at[s, t, z], lsem.at[4]
        ),
        pltpu.make_async_copy(ig_hbm, igs, lsem.at[5]),
        pltpu.make_async_copy(pg_hbm, pgs, lsem.at[6]),
    ]
    for c in loc:
        c.start()

    barrier = pltpu.get_barrier_semaphore()
    peers = (
        [{"tp": k} for k in zs] + [{"seq": k} for k in xs]
        + [{"tmpl": k} for k in ys] + [{"tmpl": tc}]
    )
    for dev in peers:
        pl.semaphore_signal(barrier, inc=1, device_id=dev, device_id_type=MESH)
    pl.semaphore_wait(barrier, len(peers))

    DN = DE // NC

    def piece(e_t, e_s, c):
        return pl.ds(pl.multiple_of((e_t * S2 + e_s) * DE + c * DN, DN), DN)

    wset = [
        (c, a, src, buf)
        for c in range(NC)
        for a, src, buf in ((1, wkv_hbm, wkv), (0, wq_hbm, wq))
    ]
    w_first = [
        queue(
            src.at[piece(t, sb, c)], buf.at[1, piece(t, sb, c)],
            r_own.at[a, c], {"tp": zp},
        )
        for c, a, src, buf in wset
    ]
    rows_first = [
        queue(tokens, xbuf.at[b], r_x.at[b], {"tp": p * h + (b + k) % h})
        for k in range(1, h)
    ]

    @pl.when(par == 0)
    def _():
        for c in w_first + rows_first:
            c.start()

    @pl.when(par == 1)
    def _():
        for c in rows_first + w_first:
            c.start()

    for k in xs:
        send(cache_hbm, cbuf.at[s], r_c.at[s], {"seq": k})
    for k in zs:
        send(
            oproj_hbm.at[pl.ds(pl.multiple_of(t * OR, OR), OR)], og.at[s, t, z],
            r_oz.at[z], {"tp": k},
        )

    GN = N // NG
    gz, zl = z // GN, z % GN
    OH = OR // 2

    def op_full(ps, pt, g):
        return og.at[ps, pt, pl.ds(g * GN, GN)]

    def op_half(ps, pt, g, f):
        return og.at[ps, pt, pl.ds(g * GN, GN), pl.ds(f * OH, OH)]

    def out_own(j):
        g = (gz + j) % NG
        for k in range(1 if j == 0 else 0, GN):
            n = g * GN + (zl + k) % GN
            arrived(og.at[s, t, n], r_oz.at[n])
        pc = op_full(s, t, g)
        for k in xs:
            send(pc, pc, r_o.at[0, s, t, g], {"seq": k})
        for k in ys:
            send(pc, pc, r_o.at[0, s, t, g], {"tmpl": k})
        send(pc, pc, r_o.at[0, s, t, g], {"tmpl": tc})

    def out_second(j):
        g = (gz + j) % NG
        for kt in ys:
            pc = op_full(s, kt, g)
            arrived(pc, r_o.at[0, s, kt, g])
            hf = op_half(s, kt, g, 0)
            for k in xs:
                send(hf, hf, r_o.at[0, s, kt, g], {"seq": k})
            send(pc, pc, r_o.at[0, s, kt, g], {"tmpl": tc})
        for ks in xs:
            pc = op_full(ks, t, g)
            arrived(pc, r_o.at[0, ks, t, g])
            hf = op_half(ks, t, g, 1)
            for k in ys:
                send(hf, hf, r_o.at[1, ks, t, g], {"tmpl": k})
            send(pc, pc, r_o.at[0, ks, t, g], {"tmpl": tc})

    def out_third(j):
        g = (gz + j) % NG
        for ks in xs:
            for kt in ys:
                for f in range(2):
                    hf = op_half(ks, kt, g, f)
                    arrived(hf, r_o.at[f, ks, kt, g])
                    send(hf, hf, r_o.at[f, ks, kt, g], {"tmpl": tc})

    def out_last(j):
        g = (gz + j) % NG
        for i in range(S):
            for m in range(T // 2):
                ks, kt = (s + i) % S, (tc + 2 * m) % T
                if i and m:
                    for f in range(2):
                        arrived(op_half(ks, kt, g, f), r_o.at[f, ks, kt, g])
                else:
                    arrived(op_full(ks, kt, g), r_o.at[0, ks, kt, g])

    loc[4].wait()
    if GN == 1:
        out_own(0)

    lens = [lengths[k] for k in range(S)]
    offs = []
    total = jnp.int32(0)
    for k in range(S):
        offs.append(total)
        total = total + lens[k]
    own_off = jnp.int32(0)
    own_len = jnp.int32(0)
    for k in range(S):
        own_off = own_off + jnp.where(s == k, offs[k], 0)
        own_len = own_len + jnp.where(s == k, lens[k], 0)

    RB = 16 if R % 16 == 0 else 8
    KC = chunk_of(D, 1024)

    def norm_rows(slot):
        def body(i, carry):
            rows = pl.ds(pl.multiple_of(i * RB, RB), RB)
            v = xbuf[slot, rows, :].astype(F32)
            inv = lax.rsqrt(jnp.sum(v * v, axis=1, keepdims=True) * (1.0 / D) + EPSILON)
            nbuf[slot, rows, :] = (v * inv * igain[...]).astype(BF16)
            return carry

        lax.fori_loop(0, R // RB, body, 0)

    def head_norm(v, gain):
        inv = lax.rsqrt(jnp.mean(v * v, axis=1, keepdims=True) + EPSILON)
        return v * inv * gain

    def project(slot, j):
        def body(i, acc):
            ks = pl.ds(pl.multiple_of(i * KC, KC), KC)
            xv = nbuf[slot, :, ks]
            return (
                acc[0] + jnp.dot(xv, wq[j, ks, :], preferred_element_type=F32),
                acc[1] + jnp.dot(xv, wkv[j, ks, :], preferred_element_type=F32),
            )

        qr, kv = lax.fori_loop(
            0, D // KC, body, (jnp.zeros((R, HW), F32), jnp.zeros((R, 2 * HW), F32))
        )
        co, si = cos_t[slot], sin_t[slot]

        def rope(u):
            return u * co + pltpu.roll(u, HW // 2, 1) * si

        q = (rope(head_norm(qr, qgain[...])) * QUERY_SCALE).astype(BF16)
        k = rope(head_norm(kv[:, :HW], kgain[...])).astype(BF16)
        return q, jnp.concatenate([k, kv[:, HW:].astype(BF16)], axis=1)

    def own_head(slot):
        q, kv = project(slot, 0)
        n = p * h + slot
        q_all[n] = q
        kv_all[s, n] = kv
        for k in xs:
            send(kv_all.at[s, n], kv_all.at[s, n], r_kvx.at[s, n], {"seq": k})

    def other_head(slot):
        q, kv = project(slot, 1)
        n = p * h + slot
        q_snd[slot] = q
        kv_snd[slot] = kv
        send(kv_snd.at[slot], kv_all.at[s, n], r_kv.at[n], {"tp": zp})
        send(q_snd.at[slot], q_all.at[n], r_q.at[n], {"tp": zp})

    loc[5].wait()
    loc[6].wait()
    for k in range(D // 128):
        igain[0:1, k * 128 : (k + 1) * 128] = igs[k : k + 1, :]
        pgain[0:1, k * 128 : (k + 1) * 128] = pgs[k : k + 1, :]
    lane = lax.broadcasted_iota(jnp.int32, (R, HW), 1)
    for k in range(h):
        row = lax.broadcasted_iota(jnp.int32, (R, HW), 0)
        angle = (PREFIX + own_off + (p * h + k) * R + row).astype(F32) * freq[...]
        cos_t[k] = jnp.cos(angle)
        sine = jnp.sin(angle)
        sin_t[k] = jnp.where(lane < HW // 2, -sine, sine)
    loc[0].wait()
    norm_rows(b)
    loc[1].wait()
    loc[2].wait()
    own_head(b)

    def w_own(c, a, src, buf):
        pc = buf.at[1, piece(t, sb, c)]
        arrived(pc, r_own.at[a, c])
        for k in x2:
            send(pc, pc, r_w.at[a, t, sb, c], {"seq": sg + k})
        for k in ys:
            send(pc, pc, r_w.at[a, t, sb, c], {"tmpl": k})
        send(pc, pc, r_w.at[a, t, sb, c], {"tmpl": tc})

    def w_x(c, a, src, buf):
        for k2 in x2:
            pc = buf.at[1, piece(t, k2, c)]
            arrived(pc, r_w.at[a, t, k2, c])
            for k in ys:
                send(pc, pc, r_w.at[a, t, k2, c], {"tmpl": k})
            send(pc, pc, r_w.at[a, t, k2, c], {"tmpl": tc})

    def w_y(c, a, src, buf):
        for k in ys:
            for k2 in range(S2):
                ks = (sb + k2) % S2
                pc = buf.at[1, piece(k, ks, c)]
                arrived(pc, r_w.at[a, k, ks, c])
                send(pc, pc, r_w.at[a, k, ks, c], {"tmpl": tc})

    for i in range(NC + 1):
        if i < NC:
            for w in wset[2 * i : 2 * i + 2]:
                w_own(*w)
        if i == 0 and GN == 1:
            out_second(0)
        if i > 0:
            for w in wset[2 * i - 2 : 2 * i]:
                w_x(*w)
    for w in wset:
        w_y(*w)

    for k in range(1, h):
        slot = (b + k) % h
        arrived(xbuf.at[slot], r_x.at[slot])
        norm_rows(slot)
        own_head(slot)
    for c, a, src, buf in wset:
        for k in range(T // 2):
            kt = (1 - par) + 2 * k
            for ks in range(S2):
                arrived(buf.at[1, piece(kt, ks, c)], r_w.at[a, kt, ks, c])
    for k in range(h):
        other_head((b + k) % h)

    for j in range(1 if GN == 1 else 0, NG):
        out_own(j)

    op = 1 - p
    for i in range(h):
        n = op * h + i
        arrived(kv_all.at[s, n], r_kv.at[n])
        for k in xs:
            send(kv_all.at[s, n], kv_all.at[s, n], r_kvx.at[s, n], {"seq": k})
    for i in range(h):
        n = op * h + i
        arrived(q_all.at[n], r_q.at[n])
    for j in range(1 if GN == 1 else 0, NG):
        out_second(j)
    loc[3].wait()
    for k in xs:
        arrived(cbuf.at[k], r_c.at[k])
        for n in range(N):
            arrived(kv_all.at[k, n], r_kvx.at[k, n])

    def attend(d, carry):
        n = lax.rem(z + d, N)
        q = q_all[n]
        slot_c = n * R + lax.broadcasted_iota(jnp.int32, (R, 1), 0)
        pos = PREFIX + own_off + slot_c
        scores, allow, values = [], [], []
        for k in range(S):
            cb = cbuf[k]
            sc = lax.dot_general(
                q, cb[:, :HW], (((1,), (1,)), ((), ())), preferred_element_type=F32
            )
            kp = PREFIX - WIN + k * C + lax.broadcasted_iota(jnp.int32, (1, C), 1)
            ok = (kp <= pos) & (kp > pos - WIN)
            scores.append(jnp.where(ok, sc, MASKED))
            allow.append(ok)
            values.append(cb[:, HW:])
            kv = flat(kv_all[k])
            sc = lax.dot_general(
                q, kv[:, :HW], (((1,), (1,)), ((), ())), preferred_element_type=F32
            )
            j = lax.broadcasted_iota(jnp.int32, (1, N * R), 1)
            kp = PREFIX + offs[k] + j
            ok = (kp <= pos) & (kp > pos - WIN) & (j < lens[k])
            scores.append(jnp.where(ok, sc, MASKED))
            allow.append(ok)
            values.append(kv[:, HW:])
        top = functools.reduce(
            jnp.maximum, [jnp.max(v, axis=1, keepdims=True) for v in scores]
        )
        row_sum = jnp.zeros((R, 1), F32)
        acc = jnp.zeros((R, HW), F32)
        for sc, ok, vv in zip(scores, allow, values):
            w = jnp.where(ok, jnp.exp(sc - top), 0.0)
            row_sum = row_sum + jnp.sum(w, axis=1, keepdims=True)
            acc = acc + jnp.dot(w.astype(BF16), vv, preferred_element_type=F32)
        live = slot_c < own_len
        res = acc / jnp.where(live, row_sum, 1.0)
        hsnd[n] = jnp.where(live, res, 0.0).astype(BF16)

        @pl.when(d < N)
        def _():
            pltpu.make_async_remote_copy(
                src_ref=hsnd.at[n], dst_ref=ho.at[z], send_sem=hssem.at[n],
                recv_sem=r_h.at[z], device_id={"tp": n}, device_id_type=MESH,
            ).start()

        return carry

    lax.fori_loop(1, N + 1, attend, 0)
    ho[z] = hsnd[z]

    for j in range(NG):
        out_third(j)
    for j in range(NG):
        out_last(j)
    for k in zs:
        arrived(ho.at[k], r_h.at[k])

    CC = chunk_of(DC, 1024)

    for k in range(S):
        def cols(i, carry):
            cs = pl.ds(pl.multiple_of(i * CC, CC), CC)
            acc = jnp.zeros((R, CC), F32)
            for g in range(N):
                w = jnp.concatenate([og[k, kt, g, :, cs] for kt in range(T)], axis=0)
                acc = acc + jnp.dot(ho[g], w, preferred_element_type=F32).astype(BF16).astype(F32)
            proj[:, pl.ds(pl.multiple_of(k * DC + i * CC, 128), CC)] = acc
            return carry

        lax.fori_loop(0, DC // CC, cols, 0)

    def finish(i, carry):
        rows = pl.ds(pl.multiple_of(i * RB, RB), RB)
        v = proj[rows, :]
        inv = lax.rsqrt(jnp.sum(v * v, axis=1, keepdims=True) * (1.0 / D) + EPSILON)
        out_ref[rows, :] = (xbuf[b, rows, :].astype(F32) + v * inv * pgain[...]).astype(BF16)
        return carry

    lax.fori_loop(0, R // RB, finish, 0)

    for c in pending:
        c.wait_send()
    for k in zs:
        pltpu.make_async_remote_copy(
            src_ref=hsnd.at[k], dst_ref=ho.at[z], send_sem=hssem.at[k],
            recv_sem=r_h.at[z], device_id={"tp": k}, device_id_type=MESH,
        ).wait_send()


def shards(
    T, S, N,
    tokens, lengths, input_gain, query_proj, key_value, query_gain, key_gain,
    window_cache, output_proj, post_gain,
):
    R, D = tokens.shape
    HW = query_proj.shape[1]
    C = window_cache.shape[0]
    h = N // 2
    S2 = max(d for d in range(1, S + 1) if S % d == 0 and D % (16 * T * d) == 0)
    NC = max(d for d in (1, 2, 3) if D // (T * S2) % (16 * d) == 0)
    NG = max(d for d in (1, 2, 4) if N % d == 0)
    inv = np.power(ROPE_BASE, -2.0 * np.arange(HW // 2) / HW)
    freq = np.concatenate([inv, inv])[None, :].astype(np.float32)
    OR, DC = output_proj.shape[0] // T, output_proj.shape[1]
    Y = T // 2 - 1
    w_sends = 2 * NC * (1 + (S2 + Y) + (S2 - 1) * (Y + 1) + Y * S2)
    o_sends = (N - 1) + NG * ((S + Y) + Y * S + (S - 1) * (Y + 1) + 2 * (S - 1) * Y)
    sends = w_sends + o_sends + (h - 1) + (S - 1) + N * (S - 1) + 2 * h
    held = 3 * h * R * D * 2 + 6 * D * HW * 2 + 2 * S * C * HW * 2 + S * T * N * OR * DC * 2
    held += (6 + 2 * S) * N * R * HW * 2 + R * D * 4 + R * D * 2
    vm = pl.BlockSpec(memory_space=pltpu.VMEM)
    hb = pl.BlockSpec(memory_space=pltpu.HBM)
    dma = pltpu.SemaphoreType.DMA
    return pl.pallas_call(
        functools.partial(kernel, T, S, N, S2, NC, NG),
        out_shape=jax.ShapeDtypeStruct((R, D), BF16),
        in_specs=[pl.BlockSpec(memory_space=pltpu.SMEM), hb, hb, hb, hb, hb]
        + [hb, hb, vm, vm, vm],
        out_specs=vm,
        scratch_shapes=[
            pltpu.VMEM((D // 128, 128), F32),
            pltpu.VMEM((D // 128, 128), F32),
            pltpu.VMEM((1, D), F32),
            pltpu.VMEM((1, D), F32),
            pltpu.VMEM((h, R, HW), F32),
            pltpu.VMEM((h, R, HW), F32),
            pltpu.VMEM((h, R, D), BF16),
            pltpu.VMEM((h, R, D), BF16),
            pltpu.VMEM((2, D, HW), BF16),
            pltpu.VMEM((2, D, 2 * HW), BF16),
            pltpu.VMEM((S, C, 2 * HW), BF16),
            pltpu.VMEM((S, T, N, OR, DC), BF16),
            pltpu.VMEM((N, R, HW), BF16),
            pltpu.VMEM((S, N, R, 2 * HW), BF16),
            pltpu.VMEM((h, R, HW), BF16),
            pltpu.VMEM((h, R, 2 * HW), BF16),
            pltpu.VMEM((N, R, HW), BF16),
            pltpu.VMEM((N, R, HW), BF16),
            pltpu.VMEM((R, D), F32),
            dma((7,)), dma((sends,)), dma((N,)),
            dma((h,)), dma((S,)), dma((2, T, S2, NC)), dma((N,)), dma((2, S, T, NG)),
            dma((N,)), dma((N,)), dma((S, N)), dma((N,)), dma((2, NC)),
        ],
        compiler_params=pltpu.CompilerParams(
            collective_id=0, has_side_effects=True, vmem_limit_bytes=held + 10 * 2**20
        ),
    )(
        lengths, tokens, query_proj, key_value, window_cache, output_proj,
        input_gain.reshape(D // 128, 128), post_gain.reshape(D // 128, 128),
        query_gain[None, :], key_gain[None, :], jnp.asarray(freq),
    )


def solution(mesh):
    T, S, N = mesh.shape["tmpl"], mesh.shape["seq"], mesh.shape["tp"]
    return jax.shard_map(
        functools.partial(shards, T, S, N),
        mesh=mesh,
        in_specs=(
            P(("tmpl", "seq", "tp"), None),
            P("tmpl"),
            P(),
            P(None, "tp"),
            P(None, "tp"),
            P(),
            P(),
            P(("tmpl", "seq"), "tp"),
            P("tp", "seq"),
            P(),
        ),
        out_specs=P(("tmpl", "seq", "tp"), None),
        check_vma=False,
    )
```

time: 105 us -> 94.5 us (0.900)
  Pallas kernels: 96.6 us -> 81.9 us
  local copies, waits for them, and re-layouts: 4.95 us -> 11.4 us
  other arithmetic: 2.54 us -> 0 us
    pallas_call x1, Pallas kernels: 96.6 us -> 81.9 us  [shards(): pl.pallas_call(functools.partial(kernel, T, S, N, S2, NC, NG), out_shape=...]
    unnamed x1 -> x23, local copies, waits for them, and re-layouts: 2.25 us -> 11.4 us
    broadcast_in_dim x2 -> x0, local copies, waits for them, and re-layouts: 2.7 us -> none  [the longest x1 1.35 us: shards(): input_gain[None, :]]
    reduce_sum x1 -> x0, other arithmetic: 1.29 us -> none  [shards(): jnp.sum(jnp.where(jnp.arange(S, dtype=jnp.int32) < s, lengths, 0))]
where the time goes in v2:
time: 94.5 us; the launch traced here: 93.3 us
  Pallas kernels  81.9 us (87%)
  local copies, waits for them, and re-layouts  11.4 us (12%)
    pallas_call x1, Pallas kernels, shards(): pl.pallas_call(functools.partial(kernel, T, S, N, S2, NC, NG), out_shape=...  81.9 us
    unnamed x23, local copies, waits for them, and re-layouts  11.4 us

profile of v2, /device:TPU:0, one launch (start us, length us, event | category | flops | bytes accessed | tf_op | source)
XLA Modules:
  0.0 93.3 jit_solution(4320967631328363268)
XLA Ops:
  0.0 0.0 copy-start
  0.0 1.8 %copy-done = bf16[5376,256]{1,0:T(8,128)(2,1)S(1)} copy-done((bf16[5376,256]{1,0:T(8,128)(2,1)S(1)}, bf16[5376,256]{1,0:T(8,128)(2,1)}, u32[]{:S(2)}) %copy-start) | copy-done | bytes 2752536
  1.8 0.0 copy-start.1
  1.8 1.3 %copy-done.1 = bf16[5376,128]{1,0:T(8,128)(2,1)S(1)} copy-done((bf16[5376,128]{1,0:T(8,128)(2,1)S(1)}, bf16[5376,128]{1,0:T(8,128)(2,1)}, u32[]{:S(2)}) %copy-start.1) | copy-done | bytes 1376280
  3.1 0.0 copy-start.2
  3.1 1.2 %copy-done.2 = bf16[96,5376]{1,0:T(8,128)(2,1)S(1)} copy-done((bf16[96,5376]{1,0:T(8,128)(2,1)S(1)}, bf16[96,5376]{1,0:T(8,128)(2,1)}, u32[]{:S(2)}) %copy-start.2) | copy-done | bytes 1032216
  4.3 0.0 copy-start.3
  4.3 1.1 %copy-done.3 = bf16[128,2688]{1,0:T(8,128)(2,1)S(1)} copy-done((bf16[128,2688]{1,0:T(8,128)(2,1)S(1)}, bf16[128,2688]{1,0:T(8,128)(2,1)}, u32[]{:S(2)}) %copy-start.3) | copy-done | bytes 688152
  5.4 0.0 copy-start.4
  5.4 0.9 %copy-done.4 = bf16[512,256]{1,0:T(8,128)(2,1)S(1)} copy-done((bf16[512,256]{1,0:T(8,128)(2,1)S(1)}, bf16[512,256]{1,0:T(8,128)(2,1)}, u32[]{:S(2)}) %copy-start.4) | copy-done | bytes 262168
  6.4 0.0 copy-start.5
  6.4 0.7 copy-done.5
  7.1 0.0 copy-start.6
  7.1 0.7 copy-done.6
  7.9 0.0 copy-start.7
  7.9 0.7 copy-done.7
  8.5 0.0 copy-start.8
  8.5 0.7 copy-done.8
  9.2 0.0 copy-start.9
  9.2 0.7 copy-done.9
  9.8 0.0 copy-start.10
  9.8 0.7 copy-done.10
  10.5 81.9 %shard_map.109 = bf16[96,5376]{1,0:T(8,128)(2,1)S(1)} custom-call(s32[2]{0:T(128)S(1)} %copy-done.7, bf16[96,5376]{1,0:T(8,128)(2,1)S(1)} %copy-done.2, bf16[5376,128]{1,0:T(8,128)(2,1)S(1)} %copy-done.1, bf16[5376,256]{1,0:T(8,128)(2,1)S(1)} %copy-done, bf16[512,256]{1,0:T(8,128)(2,1)S(1)} %copy-done.4, bf16[128,2688]{1,0:T(8,128)(2,1)S(1)} %copy-done.3, ...), custom_call_target="tpu_custom_call" | custom-call | tf_op jit(solution)/shard_map/pallas_call | solution.py:477
  92.4 1.0 %copy.13 = bf16[96,5376]{1,0:T(8,128)(2,1)} copy(bf16[96,5376]{1,0:T(8,128)(2,1)S(1)} %shard_map.109) | data formatting | bytes 2064384
Async XLA Ops:
  0.0 1.8 %copy-start = (bf16[5376,256]{1,0:T(8,128)(2,1)S(1)}, bf16[5376,256]{1,0:T(8,128)(2,1)}, u32[]{:S(2)}) copy-start(bf16[5376,256]{1,0:T(8,128)(2,1)} %wkv_hbm.1) | copy-start | bytes 8257540
  1.8 1.3 %copy-start.1 = (bf16[5376,128]{1,0:T(8,128)(2,1)S(1)}, bf16[5376,128]{1,0:T(8,128)(2,1)}, u32[]{:S(2)}) copy-start(bf16[5376,128]{1,0:T(8,128)(2,1)} %wq_hbm.1) | copy-start | bytes 4128772
  3.1 1.2 %copy-start.2 = (bf16[96,5376]{1,0:T(8,128)(2,1)S(1)}, bf16[96,5376]{1,0:T(8,128)(2,1)}, u32[]{:S(2)}) copy-start(bf16[96,5376]{1,0:T(8,128)(2,1)} %tokens.1) | copy-start | bytes 3096580
  4.3 1.1 %copy-start.3 = (bf16[128,2688]{1,0:T(8,128)(2,1)S(1)}, bf16[128,2688]{1,0:T(8,128)(2,1)}, u32[]{:S(2)}) copy-start(bf16[128,2688]{1,0:T(8,128)(2,1)} %oproj_hbm.1) | copy-start | bytes 2064388
  5.4 0.9 %copy-start.4 = (bf16[512,256]{1,0:T(8,128)(2,1)S(1)}, bf16[512,256]{1,0:T(8,128)(2,1)}, u32[]{:S(2)}) copy-start(bf16[512,256]{1,0:T(8,128)(2,1)} %cache_hbm.1) | copy-start | bytes 786436
  6.4 0.7 copy-start.5
  7.1 0.7 copy-start.6
  7.9 0.7 copy-start.7
  8.5 0.7 copy-start.8
  9.2 0.7 copy-start.9
  9.8 0.7 copy-start.10

commit v3 on v2

--- a/solution.py
+++ b/solution.py
@@ -125,23 +125,26 @@
         for k in range(1, h)
     ]
 
-    @pl.when(par == 0)
-    def _():
-        for c in w_first + rows_first:
-            c.start()
-
-    @pl.when(par == 1)
-    def _():
-        for c in rows_first + w_first:
-            c.start()
-
-    for k in xs:
-        send(cache_hbm, cbuf.at[s], r_c.at[s], {"seq": k})
-    for k in zs:
-        send(
+    out_first = [
+        queue(
             oproj_hbm.at[pl.ds(pl.multiple_of(t * OR, OR), OR)], og.at[s, t, z],
             r_oz.at[z], {"tp": k},
         )
+        for k in zs
+    ]
+
+    @pl.when(par == 0)
+    def _():
+        for c in w_first + out_first + rows_first:
+            c.start()
+
+    @pl.when(par == 1)
+    def _():
+        for c in rows_first + w_first + out_first:
+            c.start()
+
+    for k in xs:
+        send(cache_hbm, cbuf.at[s], r_c.at[s], {"seq": k})
 
     GN = N // NG
     gz, zl = z // GN, z % GN
@@ -235,37 +238,42 @@
         inv = lax.rsqrt(jnp.mean(v * v, axis=1, keepdims=True) + EPSILON)
         return v * inv * gain
 
-    def project(slot, j):
+    def project(slots, j):
         def body(i, acc):
             ks = pl.ds(pl.multiple_of(i * KC, KC), KC)
-            xv = nbuf[slot, :, ks]
+            xv = [nbuf[slot, :, ks] for slot in slots]
+            xv = jnp.concatenate(xv, axis=0) if len(slots) > 1 else xv[0]
             return (
                 acc[0] + jnp.dot(xv, wq[j, ks, :], preferred_element_type=F32),
                 acc[1] + jnp.dot(xv, wkv[j, ks, :], preferred_element_type=F32),
             )
 
+        M = R * len(slots)
         qr, kv = lax.fori_loop(
-            0, D // KC, body, (jnp.zeros((R, HW), F32), jnp.zeros((R, 2 * HW), F32))
+            0, D // KC, body, (jnp.zeros((M, HW), F32), jnp.zeros((M, 2 * HW), F32))
         )
-        co, si = cos_t[slot], sin_t[slot]
-
-        def rope(u):
-            return u * co + pltpu.roll(u, HW // 2, 1) * si
-
-        q = (rope(head_norm(qr, qgain[...])) * QUERY_SCALE).astype(BF16)
-        k = rope(head_norm(kv[:, :HW], kgain[...])).astype(BF16)
-        return q, jnp.concatenate([k, kv[:, HW:].astype(BF16)], axis=1)
+        out = []
+        for i, slot in enumerate(slots):
+            co, si = cos_t[slot], sin_t[slot]
+            rows = slice(i * R, (i + 1) * R)
+
+            def rope(u):
+                return u * co + pltpu.roll(u, HW // 2, 1) * si
+
+            q = (rope(head_norm(qr[rows], qgain[...])) * QUERY_SCALE).astype(BF16)
+            k = rope(head_norm(kv[rows, :HW], kgain[...])).astype(BF16)
+            out.append((q, jnp.concatenate([k, kv[rows, HW:].astype(BF16)], axis=1)))
+        return out
 
     def own_head(slot):
-        q, kv = project(slot, 0)
+        q, kv = project([slot], 0)[0]
         n = p * h + slot
         q_all[n] = q
         kv_all[s, n] = kv
         for k in xs:
             send(kv_all.at[s, n], kv_all.at[s, n], r_kvx.at[s, n], {"seq": k})
 
-    def other_head(slot):
-        q, kv = project(slot, 1)
+    def other_head(slot, q, kv):
         n = p * h + slot
         q_snd[slot] = q
         kv_snd[slot] = kv
@@ -324,6 +332,9 @@
         if i > 0:
             for w in wset[2 * i - 2 : 2 * i]:
                 w_x(*w)
+    for j in range(1 if GN == 1 else 0, NG):
+        out_own(j)
+
     for w in wset:
         w_y(*w)
 
@@ -337,11 +348,12 @@
             kt = (1 - par) + 2 * k
             for ks in range(S2):
                 arrived(buf.at[1, piece(kt, ks, c)], r_w.at[a, kt, ks, c])
+    if R % 16 == 0:
+        done = project(list(range(h)), 1)
+    else:
+        done = [project([k], 1)[0] for k in range(h)]
     for k in range(h):
-        other_head((b + k) % h)
-
-    for j in range(1 if GN == 1 else 0, NG):
-        out_own(j)
+        other_head(k, *done[k])
 
     op = 1 - p
     for i in range(h):
@@ -460,7 +472,7 @@
     C = window_cache.shape[0]
     h = N // 2
     S2 = max(d for d in range(1, S + 1) if S % d == 0 and D % (16 * T * d) == 0)
-    NC = max(d for d in (1, 2, 3) if D // (T * S2) % (16 * d) == 0)
+    NC = max(d for d in (1, 2, 3, 6) if D // (T * S2) % (16 * d) == 0)
     NG = max(d for d in (1, 2, 4) if N % d == 0)
     inv = np.power(ROPE_BASE, -2.0 * np.arange(HW // 2) / HW)
     freq = np.concatenate([inv, inv])[None, :].astype(np.float32)
@@ -505,7 +517,7 @@
             dma((N,)), dma((N,)), dma((S, N)), dma((N,)), dma((2, NC)),
         ],
         compiler_params=pltpu.CompilerParams(
-            collective_id=0, has_side_effects=True, vmem_limit_bytes=held + 10 * 2**20
+            collective_id=0, has_side_effects=True, vmem_limit_bytes=67043328 - 2 * R * D * 2
         ),
     )(
         lengths, tokens, query_proj, key_value, window_cache, output_proj,

time: 94.5 us -> 83.2 us (0.88)
  local copies, waits for them, and re-layouts: 11.4 us -> 2.25 us
  Pallas kernels: 81.9 us -> 79.8 us
    unnamed x23 -> x1, local copies, waits for them, and re-layouts: 11.4 us -> 2.25 us
    pallas_call x1, Pallas kernels: 81.9 us -> 79.8 us  [shards(): pl.pallas_call(functools.partial(kernel, T, S, N, S2, NC, NG), out_shape=...]
where the time goes in v3:
time: 83.2 us; the launch traced here: 82 us
  Pallas kernels  79.8 us (96%)
  local copies, waits for them, and re-layouts  2.25 us (3%)
    pallas_call x1, Pallas kernels, shards(): pl.pallas_call(functools.partial(kernel, T, S, N, S2, NC, NG), out_shape=...  79.8 us
    unnamed x1, local copies, waits for them, and re-layouts  2.25 us

profile of v3, /device:TPU:0, one launch (start us, length us, event | category | flops | bytes accessed | tf_op | source)
XLA Modules:
  0.0 82.0 jit_solution(628191981790466497)
XLA Ops:
  0.0 79.8 %shard_map.109 = bf16[96,5376]{1,0:T(8,128)(2,1)} custom-call(s32[2]{0:T(128)} %lengths.1, bf16[96,5376]{1,0:T(8,128)(2,1)} %tokens.1, bf16[5376,128]{1,0:T(8,128)(2,1)} %wq_hbm.1, bf16[5376,256]{1,0:T(8,128)(2,1)} %wkv_hbm.1, bf16[512,256]{1,0:T(8,128)(2,1)} %cache_hbm.1, bf16[128,2688]{1,0:T(8,128)(2,1)} %oproj_hbm.1, f32[42,128]{1,0:T(8,128)} %bitcast.4, ...), custom_call_target="tpu_custom_call" | custom-call | tf_op jit(solution)/shard_map/pallas_call | solution.py:489
  79.8 2.2 %copy.13 = bf16[96,5376]{1,0:T(8,128)(2,1)} copy(bf16[96,5376]{1,0:T(8,128)(2,1)} %shard_map.109) | data formatting | bytes 2064384
